TPU v7x, 256 devices: a whole 4x4x8 slice. The times are simulated.
256 devices in a mesh: own: 2 (over y_hi), space: 128 (over z, x, y_lo, core).
Axes of the slice: x: 4, y: 4 (y_hi: 2, y_lo: 2; y = y_hi * 2 + y_lo), z: 8, core: 2. Of those that a mesh axis runs over, the one named last changes fastest.
Arguments:
- density: bfloat16 [256, 4, 512, 128], P(None, 'own', 'space'), may hold values from -6 to 6
- cotangent: bfloat16 [256, 4, 512, 128], P(None, 'own', 'space'), may hold values from -6 to 6
- pw_one: bfloat16 [256, 256], P('own'), may hold values from -0.375 to 0.375
- pw_two: bfloat16 [256, 256], P('own'), may hold values from -0.375 to 0.375
- dw_one: bfloat16 [27, 256], P(None, 'own'), may hold values from -1.25 to 1.25
- dw_two: bfloat16 [27, 256], P(None, 'own'), may hold values from -1.25 to 1.25
Outputs:
- grad_input: bfloat16 [256, 4, 512, 128], P(None, 'own', 'space')
- grad_pw_one: float32 [256, 256], P('own')
- grad_pw_two: float32 [256, 256], P('own')
- grad_dw_one: float32 [27, 256], P(None, 'own')
- grad_dw_two: float32 [27, 256], P(None, 'own')
All inputs are finite; a program needn't handle non-finite values.
Results may differ from a plain program's by a relative error of at most 0.01.
Values may be sent and summed in bfloat16 or wider, within the bound.
A program may use at most 192 MiB of HBM per device.

v0:
```python
import math
import jax
import jax.numpy as jnp
from jax import lax
from jax.sharding import PartitionSpec as P

TAP_LIST = [
    (9 * (a + 1) + 3 * (b + 1) + (d + 1), a, b, d)
    for a in (-1, 0, 1)
    for b in (-1, 0, 1)
    for d in (-1, 0, 1)
]


def extended(value, sides, width):
    for axis, dim in sides:
        size, length = (lax.axis_size(axis), value.shape[dim])
        up = [(i, (i + 1) % size) for i in range(size)]
        down = [(j, i) for i, j in up]
        last = lax.slice_in_dim(value, length - width, length, axis=dim)
        first = lax.slice_in_dim(value, 0, width, axis=dim)
        before = lax.ppermute(last, axis, up)
        after = lax.ppermute(first, axis, down)
        value = jnp.concatenate([before, value, after], axis=dim)
    return value


def depthwise(padded, weights, extent_x, extent_y, direction):
    running = jnp.zeros((padded.shape[0], extent_x, extent_y, padded.shape[3]), jnp.float32)
    for k, a, b, d in TAP_LIST:
        start_x = 1 + direction * a
        start_y = 1 + direction * b
        shifted = padded[:, start_x : start_x + extent_x, start_y : start_y + extent_y, :]
        shifted = jnp.roll(shifted, -direction * d, axis=3).astype(jnp.float32)
        running = running + weights[k].astype(jnp.float32)[:, None, None, None] * shifted
    return running


def tap_sums(padded, gradient):
    extent_x = gradient.shape[1]
    extent_y = gradient.shape[2]
    grad_float = gradient.astype(jnp.float32)
    columns = []
    for k, a, b, d in TAP_LIST:
        shifted = padded[:, 1 + a : 1 + a + extent_x, 1 + b : 1 + b + extent_y, :]
        shifted = jnp.roll(shifted, -d, axis=3).astype(jnp.float32)
        columns.append(jnp.sum(shifted * grad_float, axis=(1, 2, 3)))
    return jnp.stack(columns, axis=0)


def pointwise(weights, source):
    layout = source.shape
    flattened = source.reshape(layout[0], -1)
    return jnp.dot(weights.T, flattened, preferred_element_type=jnp.float32).reshape(layout)


def backmap(weights, source):
    layout = source.shape
    flattened = source.reshape(layout[0], -1)
    return jnp.dot(weights, flattened, preferred_element_type=jnp.float32).reshape(layout)


def contract_cells(left, right):
    channels = left.shape[0]
    return lax.dot_general(
        left.reshape(channels, -1),
        right.reshape(channels, -1),
        (((1,), (1,)), ((), ())),
        preferred_element_type=jnp.float32,
    )


def shards(density, cotangent, pw_one, pw_two, dw_one, dw_two):
    channels, extent_x, extent_y, extent_z = density.shape
    weight_one, weight_two, taps_one, taps_two = (
        lax.all_gather(pw_one, "own", axis=0, tiled=True),
        lax.all_gather(pw_two, "own", axis=0, tiled=True),
        lax.all_gather(dw_one, "own", axis=1, tiled=True),
        lax.all_gather(dw_two, "own", axis=1, tiled=True),
    )
    rim_width = 1
    wide_input = extended(density, (("own", 1), ("space", 2)), rim_width)
    first = depthwise(wide_input, taps_one, extent_x, extent_y, 1).astype(jnp.bfloat16)
    pre = pointwise(weight_one, first)
    act = jax.nn.silu(pre).astype(jnp.bfloat16)
    act_padded = extended(act, (("own", 1), ("space", 2)), 1)
    second = depthwise(act_padded, taps_two, extent_x, extent_y, 1).astype(jnp.bfloat16)
    grad_second = backmap(weight_two, cotangent).astype(jnp.bfloat16)
    second_padded = extended(grad_second, (("own", 1), ("space", 2)), 1)
    sigma = jax.nn.sigmoid(pre)
    grad_pre = (
        depthwise(second_padded, taps_two, extent_x, extent_y, -1)
        * (sigma * (1.0 + pre * (1.0 - sigma)))
    ).astype(jnp.bfloat16)
    grad_first = backmap(weight_one, grad_pre).astype(jnp.bfloat16)
    first_padded = extended(grad_first, (("own", 1), ("space", 2)), 1)
    grad_input = (
        cotangent.astype(jnp.float32) + depthwise(first_padded, taps_one, extent_x, extent_y, -1)
    ).astype(jnp.bfloat16)
    total_cells = extent_x * extent_y * extent_z * lax.axis_size("own") * lax.axis_size("space")
    grad_scale = 1.0 / math.sqrt(float(total_cells))
    local_pw_one = contract_cells(first, grad_pre) * grad_scale
    local_pw_two = contract_cells(second, cotangent) * grad_scale
    local_dw_one = tap_sums(wide_input, grad_first) * grad_scale
    local_dw_two = tap_sums(act_padded, grad_second) * grad_scale
    partials = (local_pw_one, local_pw_two, local_dw_one, local_dw_two)
    summed = lax.psum((partials[0], partials[1], partials[2], partials[3]), ("own", "space"))
    share_rows = channels // lax.axis_size("own")
    position = lax.axis_index("own") * share_rows
    result = (
        lax.dynamic_slice_in_dim(summed[0], position, share_rows, 0),
        lax.dynamic_slice_in_dim(summed[1], position, share_rows, 0),
        lax.dynamic_slice_in_dim(summed[2], position, share_rows, 1),
        lax.dynamic_slice_in_dim(summed[3], position, share_rows, 1),
    )
    return (grad_input, result[0], result[1], result[2], result[3])


def solution(mesh):
    in_specs = (
        P(None, "own", "space", None),
        P(None, "own", "space", None),
        P("own", None),
        P("own", None),
        P(None, "own"),
        P(None, "own"),
    )
    out_specs = (
        P(None, "own", "space", None),
        P("own", None),
        P("own", None),
        P(None, "own"),
        P(None, "own"),
    )
    return jax.shard_map(shards, mesh=mesh, in_specs=in_specs, out_specs=out_specs, check_vma=False)
```

profile of v0, /device:TPU:1, one launch (start us, length us, event | category | flops | bytes accessed | tf_op | source)
XLA Modules:
  0.0 458.6 jit_solution(16944286519748687142)
XLA Ops:
  7.3 1.4 copy.90
  8.7 3.8 collective-permute-start.5
  12.6 11.0 %all_gather.12 = bf16[27,256]{1,0:T(8,128)(2,1)S(1)} all-gather(bf16[27,128]{1,0:T(8,128)(2,1)S(1)} %copy-done.80), channel_id=1, replica_groups=mesh['own'=2,'space'=128] {'own'}, dimensions={1}, use_global_device_ids=true | all-gather | bytes 20736 | tf_op jit(solution)/shard_map/all_gather | solution.py:78
  23.6 0.7 slice_convert_fusion.53
  24.9 5.3 %all_gather.13 = bf16[27,256]{1,0:T(8,128)(2,1)S(1)} all-gather(bf16[27,128]{1,0:T(8,128)(2,1)S(1)} %copy-done.81), channel_id=1, replica_groups=mesh['own'=2,'space'=128] {'own'}, dimensions={1}, use_global_device_ids=true | all-gather | bytes 20736 | tf_op jit(solution)/shard_map/all_gather | solution.py:79
  30.2 0.7 slice_convert_fusion.52
  31.5 5.3 %all_gather.15 = bf16[256,256]{1,0:T(8,128)(2,1)S(1)} all-gather(bf16[128,256]{1,0:T(8,128)(2,1)S(1)} %copy-done.24), channel_id=1, replica_groups=mesh['own'=2,'space'=128] {'own'}, dimensions={0}, use_global_device_ids=true | all-gather | bytes 196608 | tf_op jit(solution)/shard_map/all_gather | solution.py:76
  37.2 1.1 copy.88
  38.3 1.0 copy.89
  39.3 5.4 %all_gather.14 = bf16[256,256]{1,0:T(8,128)(2,1)} all-gather(bf16[128,256]{1,0:T(8,128)(2,1)S(1)} %copy-done.25), channel_id=1, replica_groups=mesh['own'=2,'space'=128] {'own'}, dimensions={0}, use_global_device_ids=true | all-gather | bytes 196608 | tf_op jit(solution)/shard_map/all_gather | solution.py:77
  45.0 6.1 %collective-permute-start.6 = (bf16[256,4,1,128]{3,0,2,1:T(8,128)(2,1)S(1)}, bf16[256,4,1,128]{3,0,2,1:T(8,128)(2,1)}, u32[]{:S(2)}, u32[]{:S(2)}) collective-permute-start(bf16[256,4,1,128]{3,0,2,1:T(8,128)(2,1)S(1)} %copy.93), channel_id=1, source_target_pairs={{0,1},{1,2},{2,3},{3,4},{4,5},{5,6},{6,7},{7,8},{8,9},{9,10},{10,1... | collective-permute-start | bytes 786440 | tf_op jit(solution)/shard_map/ppermute | solution.py:22
  51.1 0.9 copy.96
  52.0 1.4 fusion.146
  53.4 2.3 fusion.217
  55.8 1.8 copy.94
  57.6 3.4 collective-permute-done.7
  60.9 1.8 copy.97
  62.7 1.2 maximum_maximum_fusion.1
  64.3 1.8 fusion.289
  66.4 11.0 %add_convert_fusion = (bf16[256,2,4,128]{0,3,2,1:T(8,128)(2,1)S(1)}, f32[256,2,4,128]{0,3,2,1:T(8,128)}, f32[256,2,4,128]{0,3,2,1:T(8,128)}, f32[256,2,4,128]{0,...) fusion(bf16[256,2,4,128]{0,3,2,1:T(8,128)(2,1)S(1)} %copy.90, ...), kind=kLoop, calls=%fused_computation.272 | loop fusion | flops 57933824 | bytes 27225088 | tf_op jit(solution)/shard_map/convert_element_type | solution.py:83
  78.7 2.6 collective-permute-start.13
  81.3 0.8 collective-permute-start.12
  82.1 1.5 maximum_convert_fusion
  83.7 2.8 collective-permute-done.13
  86.5 5.6 %collective-permute-done.12 = bf16[256,1,4,128]{0,3,2,1:T(8,128)(2,1)S(1)} collective-permute-done((bf16[256,1,4,128]{0,3,2,1:T(8,128)(2,1)S(1)}, bf16[256,1,4,128]{0,3,2,1:T(8,128)(2,1)S(1)}, u32[]{:S(2)}, u32[]{:S(2)}) %collective-permute-start.12) | collective-permute-done | bytes 262176 | tf_op jit(solution)/shard_map/ppermute | solution.py:22
  92.2 1.5 collective-permute-start.14
  93.7 1.0 collective-permute-start.15
  95.2 1.8 collective-permute-done.14
  97.1 2.5 collective-permute-done.15
  99.8 0.7 fusion.284
  100.8 2.1 fusion.120
  103.0 0.8 fusion.294
  103.8 2.9 collective-permute-start
  106.8 0.7 fusion.283
  107.5 1.4 fusion.135
  108.8 1.3 fusion.131
  110.4 2.1 fusion.136
  112.7 5.8 %fusion = f32[256,256]{1,0:T(8,128)} fusion(bf16[256,2,4,128]{0,3,2,1:T(8,128)(2,1)S(1)} %copy-done.11, bf16[256,2,4,128]{0,3,2,1:T(8,128)(2,1)S(1)} %multiply_convert_fusion, f32[256]{0:T(256)S(1)} %bitcast.317, f32[256]{0:T(256)S(1)} %bitcast.319, f32[256]{0:T(256)S(1)} %bitcast.321, f32[256]{0:T(256)S(1)} %bitcast.323, f32[256]{0:T(256)S(1)} %bitcast.325, ...), kind=kOutput, calls=%fused_computation.119 | convolution fusion | flops 192217088 | bytes 14986240 | tf_op jit(solution)/shard_map/dot_general | solution.py:65
  118.5 1.2 fusion.137
  119.7 5.2 %stack.223 = f32[27,256]{1,0:T(8,128)} concatenate(f32[1,256]{1,0:T(1,128)} %bitcast.379, f32[1,256]{1,0:T(1,128)} %bitcast.306, f32[1,256]{1,0:T(1,128)} %bitcast.380, f32[1,256]{1,0:T(1,128)} %bitcast.309, f32[1,256]{1,0:T(1,128)} %bitcast.381, f32[1,256]{1,0:T(1,128)} %bitcast.310, f32[1,256]{1,0:T(1,128)S(1)} %bitcast.275, f32[1,256]{1,0:T(1,128)} %bitcast.303, ...), dimensions={0} | concatenate | bytes 55296 | tf_op jit(solution)/shard_map/stack | solution.py:48
  125.0 1.4 broadcast_multiply_fusion
  126.4 3.4 collective-permute-start.3
  129.8 2.6 collective-permute-start.2
  132.9 3.0 collective-permute-done.3
  136.2 0.7 fusion.288
  137.2 0.7 fusion.287
  138.4 9.1 %fusion.139 = bf16[256,2,4,128]{0,3,2,1:T(8,128)(2,1)S(1)} fusion(f32[256,2,4,128]{0,3,2,1:T(8,128)S(1)} %bitcast.215, bf16[256,2,4,128]{0,3,2,1:T(8,128)(2,1)S(1)} %get-tuple-element.274, bf16[256,1,4,128]{0,3,2,1:T(8,128)(2,1)S(1)} %collective-permute-done, bf16[256,1,4,128]{0,3,2,1:T(8,128)(2,1)S(1)} %collective-permute-done.1, ...), kind=kLoop, calls=%fused_computation.274 | loop fusion | flops 58982400 | bytes 14666752 | tf_op jit(solution)/shard_map/convert_element_type | solution.py:94
  147.5 0.8 copy-done.17
  148.3 1.1 fusion.1
  149.4 8.2 %fusion.95 = (f32[256]{0:T(256)S(1)}, f32[256]{0:T(256)S(1)}, f32[256]{0:T(256)S(1)}, f32[256]{0:T(256)S(1)}, f32[256]{0:T(256)}, /*index=5*/f32[256]{0:T(256)},...) fusion(f32[256,2,4,128]{0,3,2,1:T(8,128)} %get-tuple-element.96, ...), kind=kOutput, calls=%fused_computation.227 | convolution fusion | flops 144174592 | bytes 20072448 | tf_op jit(solution)/shard_map/dot_general | solution.py:60
  157.6 0.8 fusion.293
  158.4 2.9 collective-permute-start.8
  161.5 2.3 fusion.77
  164.1 87.9 %all-reduce = (f32[27,256]{1,0:T(8,128)S(1)}, f32[27,256]{1,0:T(8,128)S(1)}) all-reduce(f32[27,256]{1,0:T(8,128)S(1)} %broadcast_multiply_fusion.1, f32[27,256]{1,0:T(8,128)S(1)} %copy-done.23), channel_id=1, replica_groups=mesh['own'=2,'space'=128] {'own','space'}, use_global_device_ids=true, to_apply=%region_29.30 | all-reduce | flops 13824 | bytes 110592 | tf_op jit(solution)/shard_map/psum | solution.py:107
  253.2 168.2 %all-reduce.4.cloned.1.call-done = (f32[256,256]{1,0:T(8,128)}, f32[256,256]{1,0:T(8,128)}) async-done(((f32[256,256]{1,0:T(8,128)}, f32[256,256]{1,0:T(8,128)}), (f32[256,256]{1,0:T(8,128)}, f32[256,256]{1,0:T(8,128)})) %all-reduce.4.cloned.1.call-update) | async-done | bytes 524304 | tf_op jit(solution)/shard_map/psum | solution.py:107
  421.4 1.6 constant_dynamic-slice_fusion.3
  423.0 1.6 constant_dynamic-slice_fusion.2
  424.8 3.3 collective-permute-start.11
  428.6 1.6 fusion.152
  430.2 1.2 collective-permute-done.11
  431.5 5.6 %collective-permute-done.10 = bf16[256,4,1,128]{3,0,2,1:T(8,128)(2,1)S(1)} collective-permute-done((bf16[256,4,1,128]{3,0,2,1:T(8,128)(2,1)S(1)}, bf16[256,4,1,128]{3,0,2,1:T(8,128)(2,1)S(1)}, u32[]{:S(2)}, u32[]{:S(2)}) %collective-permute-start.10) | collective-permute-done | bytes 262176 | tf_op jit(solution)/shard_map/ppermute | solution.py:23
  438.4 0.7 fusion.285
  440.0 9.5 %fusion.138 = bf16[256,2,4,128]{0,3,2,1:T(8,128)(2,1)} fusion(bf16[256,2,4,128]{0,3,2,1:T(8,128)(2,1)S(1)} %bitcast.213, bf16[256,2,4,128]{0,3,2,1:T(8,128)(2,1)S(1)} %copy-done.12, bf16[256,1,4,128]{0,3,2,1:T(8,128)(2,1)S(1)} %collective-permute-done.8, bf16[256,1,4,128]{0,3,2,1:T(8,128)(2,1)S(1)} %collective-permute-done.9, ...), kind=kLoop, calls=%fused_computation.273 | loop fusion | flops 57409536 | bytes 14142464 | tf_op jit(solution)/shard_map/convert_element_type | solution.py:99
  449.5 2.1 copy.112
  (344 shorter events, 9.9 us)
Async XLA Ops:
  7.2 5.4 %copy-start.80 = (bf16[27,128]{1,0:T(8,128)(2,1)S(1)}, bf16[27,128]{1,0:T(8,128)(2,1)}, u32[]{:S(2)}) copy-start(bf16[27,128]{1,0:T(8,128)(2,1)} %param.10) | copy-start | bytes 20740
  7.2 17.7 %copy-start.81 = (bf16[27,128]{1,0:T(8,128)(2,1)S(1)}, bf16[27,128]{1,0:T(8,128)(2,1)}, u32[]{:S(2)}) copy-start(bf16[27,128]{1,0:T(8,128)(2,1)} %param.11) | copy-start | bytes 20740
  7.2 24.3 %copy-start.24 = (bf16[128,256]{1,0:T(8,128)(2,1)S(1)}, bf16[128,256]{1,0:T(8,128)(2,1)}, u32[]{:S(2)}) copy-start(bf16[128,256]{1,0:T(8,128)(2,1)} %param.8) | copy-start | bytes 196612
  7.2 29.6 %copy-start.18 = (bf16[256,2,4,128]{3,2,1,0:T(4,128)(2,1)S(1)}, bf16[256,2,4,128]{3,2,1,0:T(4,128)(2,1)}, u32[]{:S(2)}) copy-start(bf16[256,2,4,128]{3,2,1,0:T(4,128)(2,1)} %param.7) | copy-start | bytes 1572868
  7.2 414.2 %all-reduce.4.cloned.1.call-start = ((), (), s32[]{:S(2)}) async-start(), calls=%async_computation | async-start | bytes 1048576 | tf_op jit(solution)/shard_map/psum | solution.py:107
  8.7 36.1 %collective-permute-start.5 = (bf16[256,1,4,128]{0,3,2,1:T(8,128)(2,1)S(1)}, bf16[256,1,4,128]{0,3,2,1:T(8,128)(2,1)S(1)}, u32[]{:S(2)}, u32[]{:S(2)}) collective-permute-start(bf16[256,1,4,128]{0,3,2,1:T(8,128)(2,1)S(1)} %get-tuple-element.218), channel_id=1, source_target_pairs={{128,0},{0,128},{129,1},{1,129},{130,2},{2,130},{131,3},{3,131},{1... | collective-permute-start | bytes 786440 | tf_op jit(solution)/shard_map/ppermute | solution.py:23
  12.5 32.3 %collective-permute-start.4 = (bf16[256,1,4,128]{0,3,2,1:T(8,128)(2,1)S(1)}, bf16[256,1,4,128]{0,3,2,1:T(8,128)(2,1)S(1)}, u32[]{:S(2)}, u32[]{:S(2)}) collective-permute-start(bf16[256,1,4,128]{0,3,2,1:T(8,128)(2,1)S(1)} %get-tuple-element.217), channel_id=1, source_target_pairs={{0,128},{128,0},{1,129},{129,1},{2,130},{130,2},{3,131},{131,3},{4... | collective-permute-start | bytes 786440 | tf_op jit(solution)/shard_map/ppermute | solution.py:22
  45.0 10.7 %collective-permute-start.6 = (bf16[256,4,1,128]{3,0,2,1:T(8,128)(2,1)S(1)}, bf16[256,4,1,128]{3,0,2,1:T(8,128)(2,1)}, u32[]{:S(2)}, u32[]{:S(2)}) collective-permute-start(bf16[256,4,1,128]{3,0,2,1:T(8,128)(2,1)S(1)} %copy.93), channel_id=1, source_target_pairs={{0,1},{1,2},{2,3},{3,4},{4,5},{5,6},{6,7},{7,8},{8,9},{9,10},{10,1... | collective-permute-start | bytes 786440 | tf_op jit(solution)/shard_map/ppermute | solution.py:22
  52.0 8.9 %collective-permute-start.7 = (bf16[256,4,1,128]{3,0,2,1:T(8,128)(2,1)}, bf16[256,4,1,128]{3,0,2,1:T(8,128)(2,1)}, u32[]{:S(2)}, u32[]{:S(2)}) collective-permute-start(bf16[256,4,1,128]{3,0,2,1:T(8,128)(2,1)} %copy.96), channel_id=1, source_target_pairs={{1,0},{2,1},{3,2},{4,3},{5,4},{6,5},{7,6},{8,7},{9,8},{10,9},{11,1... | collective-permute-start | bytes 786440 | tf_op jit(solution)/shard_map/ppermute | solution.py:23
  53.4 2.3 copy-start.3
  53.4 2.3 copy-start.5
  78.7 7.8 %collective-permute-start.13 = (bf16[256,1,4,128]{0,3,2,1:T(8,128)(2,1)S(1)}, bf16[256,1,4,128]{0,3,2,1:T(8,128)(2,1)S(1)}, u32[]{:S(2)}, u32[]{:S(2)}) collective-permute-start(bf16[256,1,4,128]{0,3,2,1:T(8,128)(2,1)S(1)} %get-tuple-element.190), channel_id=1, source_target_pairs={{128,0},{0,128},{129,1},{1,129},{130,2},{2,130},{131,3},{3,131},{1... | collective-permute-start | bytes 786440 | tf_op jit(solution)/shard_map/ppermute | solution.py:23
  81.3 10.8 %collective-permute-start.12 = (bf16[256,1,4,128]{0,3,2,1:T(8,128)(2,1)S(1)}, bf16[256,1,4,128]{0,3,2,1:T(8,128)(2,1)S(1)}, u32[]{:S(2)}, u32[]{:S(2)}) collective-permute-start(bf16[256,1,4,128]{0,3,2,1:T(8,128)(2,1)S(1)} %get-tuple-element.189), channel_id=1, source_target_pairs={{0,128},{128,0},{1,129},{129,1},{2,130},{130,2},{3,131},{131,3},{4... | collective-permute-start | bytes 786440 | tf_op jit(solution)/shard_map/ppermute | solution.py:22
  92.2 4.9 %collective-permute-start.14 = (bf16[256,4,1,128]{0,3,2,1:T(8,128)(2,1)S(1)}, bf16[256,4,1,128]{0,3,2,1:T(8,128)(2,1)S(1)}, u32[]{:S(2)}, u32[]{:S(2)}) collective-permute-start(bf16[256,4,1,128]{0,3,2,1:T(8,128)(2,1)S(1)} %get-tuple-element.147), channel_id=1, source_target_pairs={{0,1},{1,2},{2,3},{3,4},{4,5},{5,6},{6,7},{7,8},{8,9},{9,10},{10,1... | collective-permute-start | bytes 786440 | tf_op jit(solution)/shard_map/ppermute | solution.py:22
  93.7 5.8 %collective-permute-start.15 = (bf16[256,4,1,128]{0,3,2,1:T(8,128)(2,1)S(1)}, bf16[256,4,1,128]{0,3,2,1:T(8,128)(2,1)S(1)}, u32[]{:S(2)}, u32[]{:S(2)}) collective-permute-start(bf16[256,4,1,128]{0,3,2,1:T(8,128)(2,1)S(1)} %get-tuple-element.148), channel_id=1, source_target_pairs={{1,0},{2,1},{3,2},{4,3},{5,4},{6,5},{7,6},{8,7},{9,8},{10,9},{11,1... | collective-permute-start | bytes 786440 | tf_op jit(solution)/shard_map/ppermute | solution.py:23
  103.8 22.5 %collective-permute-start = (bf16[256,1,4,128]{0,3,2,1:T(8,128)(2,1)}, bf16[256,1,4,128]{0,3,2,1:T(8,128)(2,1)S(1)}, u32[]{:S(2)}, u32[]{:S(2)}) collective-permute-start(bf16[256,1,4,128]{0,3,2,1:T(8,128)(2,1)} %get-tuple-element.210), channel_id=1, source_target_pairs={{0,128},{128,0},{1,129},{129,1},{2,130},{130,2},{3,131},{131,3},{4... | collective-permute-start | bytes 786440 | tf_op jit(solution)/shard_map/ppermute | solution.py:22
  106.7 19.6 %collective-permute-start.1 = (bf16[256,1,4,128]{0,3,2,1:T(8,128)(2,1)}, bf16[256,1,4,128]{0,3,2,1:T(8,128)(2,1)S(1)}, u32[]{:S(2)}, u32[]{:S(2)}) collective-permute-start(bf16[256,1,4,128]{0,3,2,1:T(8,128)(2,1)} %get-tuple-element.209), channel_id=1, source_target_pairs={{128,0},{0,128},{129,1},{1,129},{130,2},{2,130},{131,3},{3,131},{1... | collective-permute-start | bytes 786440 | tf_op jit(solution)/shard_map/ppermute | solution.py:23
  110.1 2.3 copy-start.100
  110.1 2.3 copy-start.102
  110.2 2.3 copy-start.104
  110.2 2.3 copy-start.106
  110.2 2.3 copy-start.108
  110.2 2.3 copy-start.110
  110.2 2.3 copy-start.112
  110.2 2.3 copy-start.114
  110.2 2.3 copy-start.116
  110.2 2.3 copy-start.118
  110.2 2.3 copy-start.120
  110.2 2.3 copy-start.122
  110.3 2.3 copy-start.124
  110.3 2.3 copy-start.126
  110.3 2.3 copy-start.128
  110.3 2.3 copy-start.130
  110.3 2.3 copy-start.132
  110.3 2.3 copy-start.134
  110.3 2.3 copy-start.136
  110.3 2.3 copy-start.138
  110.3 2.3 copy-start.140
  110.3 2.3 copy-start.142
  110.4 2.3 copy-start.144
  110.4 2.3 copy-start.146
  110.4 2.3 copy-start.148
  126.4 9.6 %collective-permute-start.3 = (bf16[256,4,1,128]{0,3,2,1:T(8,128)(2,1)S(1)}, bf16[256,4,1,128]{0,3,2,1:T(8,128)(2,1)S(1)}, u32[]{:S(2)}, u32[]{:S(2)}) collective-permute-start(bf16[256,4,1,128]{0,3,2,1:T(8,128)(2,1)S(1)} %get-tuple-element.156), channel_id=1, source_target_pairs={{0,1},{1,2},{2,3},{3,4},{4,5},{5,6},{6,7},{7,8},{8,9},{9,10},{10,1... | collective-permute-start | bytes 786440 | tf_op jit(solution)/shard_map/ppermute | solution.py:22
  129.8 6.1 %collective-permute-start.2 = (bf16[256,4,1,128]{0,3,2,1:T(8,128)(2,1)S(1)}, bf16[256,4,1,128]{0,3,2,1:T(8,128)(2,1)S(1)}, u32[]{:S(2)}, u32[]{:S(2)}) collective-permute-start(bf16[256,4,1,128]{0,3,2,1:T(8,128)(2,1)S(1)} %get-tuple-element.155), channel_id=1, source_target_pairs={{1,0},{2,1},{3,2},{4,3},{5,4},{6,5},{7,6},{8,7},{9,8},{10,9},{11,1... | collective-permute-start | bytes 786440 | tf_op jit(solution)/shard_map/ppermute | solution.py:23
  138.4 9.9 %copy-start.20 = (bf16[256,2,4,128]{0,3,2,1:T(8,128)(2,1)S(1)}, bf16[256,2,4,128]{0,3,2,1:T(8,128)(2,1)}, u32[]{:S(2)}) copy-start(bf16[256,2,4,128]{0,3,2,1:T(8,128)(2,1)} %copy-done.19) | copy-start | bytes 1572868
  158.4 266.2 %collective-permute-start.8 = (bf16[256,1,4,128]{0,3,2,1:T(8,128)(2,1)}, bf16[256,1,4,128]{0,3,2,1:T(8,128)(2,1)S(1)}, u32[]{:S(2)}, u32[]{:S(2)}) collective-permute-start(bf16[256,1,4,128]{0,3,2,1:T(8,128)(2,1)} %get-tuple-element.200), channel_id=1, source_target_pairs={{0,128},{128,0},{1,129},{129,1},{2,130},{130,2},{3,131},{131,3},{4... | collective-permute-start | bytes 786440 | tf_op jit(solution)/shard_map/ppermute | solution.py:22
  161.3 263.2 %collective-permute-start.9 = (bf16[256,1,4,128]{0,3,2,1:T(8,128)(2,1)}, bf16[256,1,4,128]{0,3,2,1:T(8,128)(2,1)S(1)}, u32[]{:S(2)}, u32[]{:S(2)}) collective-permute-start(bf16[256,1,4,128]{0,3,2,1:T(8,128)(2,1)} %get-tuple-element.199), channel_id=1, source_target_pairs={{128,0},{0,128},{129,1},{1,129},{130,2},{2,130},{131,3},{3,131},{1... | collective-permute-start | bytes 786440 | tf_op jit(solution)/shard_map/ppermute | solution.py:23
  161.4 2.4 copy-start.82
  161.4 2.4 copy-start.83
  161.4 2.4 copy-start.84
  161.4 2.4 copy-start.85
  161.4 2.4 copy-start.86
  161.4 2.4 copy-start.87
  161.4 2.4 copy-start.88
  161.5 2.4 copy-start.89
  161.5 2.4 copy-start.90
  161.5 2.4 copy-start.91
  161.5 2.4 copy-start.92
  161.5 2.4 copy-start.93
  161.5 2.4 copy-start.94
  161.5 2.4 copy-start.95
  161.5 2.5 copy-start.23
  424.8 6.6 %collective-permute-start.11 = (bf16[256,4,1,128]{3,0,2,1:T(8,128)(2,1)S(1)}, bf16[256,4,1,128]{3,0,2,1:T(8,128)(2,1)S(1)}, u32[]{:S(2)}, u32[]{:S(2)}) collective-permute-start(bf16[256,4,1,128]{3,0,2,1:T(8,128)(2,1)S(1)} %copy.106), channel_id=1, source_target_pairs={{0,1},{1,2},{2,3},{3,4},{4,5},{5,6},{6,7},{7,8},{8,9},{9,10},{10,1... | collective-permute-start | bytes 786440 | tf_op jit(solution)/shard_map/ppermute | solution.py:22
  428.2 8.9 %collective-permute-start.10 = (bf16[256,4,1,128]{3,0,2,1:T(8,128)(2,1)S(1)}, bf16[256,4,1,128]{3,0,2,1:T(8,128)(2,1)S(1)}, u32[]{:S(2)}, u32[]{:S(2)}) collective-permute-start(bf16[256,4,1,128]{3,0,2,1:T(8,128)(2,1)S(1)} %copy.104), channel_id=1, source_target_pairs={{1,0},{2,1},{3,2},{4,3},{5,4},{6,5},{7,6},{8,7},{9,8},{10,9},{11,1... | collective-permute-start | bytes 786440 | tf_op jit(solution)/shard_map/ppermute | solution.py:23
  (103 other events, 170.5 us)
Sparse Core Ops, SparseCore 0:
  161.5 259.8 all-reduce.3
where the time goes:
time: 468 us; the launch traced here: 459 us
  waiting for transfers between devices  194 us (41%)
  blocking collectives  115 us (25%)
  other arithmetic  52.1 us (11%)
  local copies, waits for them, and re-layouts  31.8 us (7%)
  starting transfers between devices  31.6 us (7%)
  matrix products  17.5 us (4%)
  between operations  16.6 us (4%)
    psum x1, waiting for transfers between devices, shards(): lax.psum((partials[0], partials[1], partials[2], partials[3]), ('own', 's...  168 us
    psum x1, blocking collectives, shards(): lax.psum((partials[0], partials[1], partials[2], partials[3]), ('own', 's...  87.9 us
    ppermute x8, starting transfers between devices, extended(): before = lax.ppermute(last, axis, up)  21.1 us
    ppermute x8, waiting for transfers between devices, extended(): after = lax.ppermute(first, axis, down)  14.3 us
    ppermute x8, waiting for transfers between devices, extended(): before = lax.ppermute(last, axis, up)  11.7 us
    convert_element_type x1, other arithmetic, shards(): depthwise(wide_input, taps_one, extent_x, extent_y, 1).astype(jnp.bfloat16)  11 us
    all_gather x1, blocking collectives, shards(): lax.all_gather(dw_one, 'own', axis=1, tiled=True)  11 us
    ppermute x8, starting transfers between devices, extended(): after = lax.ppermute(first, axis, down)  10.5 us
  transfers between devices with their start and end apart: 17, of which 9 were waited for; matrix products, arithmetic and copies ran while one was open for 9% of the time, Pallas kernels for 0%

commit v1 on v0

--- a/solution.py
+++ b/solution.py
@@ -104,7 +104,8 @@
     local_dw_one = tap_sums(wide_input, grad_first) * grad_scale
     local_dw_two = tap_sums(act_padded, grad_second) * grad_scale
     partials = (local_pw_one, local_pw_two, local_dw_one, local_dw_two)
-    summed = lax.psum((partials[0], partials[1], partials[2], partials[3]), ("own", "space"))
+    one_axis = lax.psum((partials[0], partials[1], partials[2], partials[3]), "own")
+    summed = lax.psum(one_axis, "space")
     share_rows = channels // lax.axis_size("own")
     position = lax.axis_index("own") * share_rows
     result = (

time: 468 us -> 1770 us (3.78)
  waiting for transfers between devices: 194 us -> 1010 us
  blocking collectives: 115 us -> 593 us
    psum x1 -> x2, waiting for transfers between devices: 168 us -> 993 us  [the longest x1 993 us: shards(): summed = lax.psum(one_axis, 'space')]
    psum x1 -> x2, blocking collectives: 87.9 us -> 566 us  [the longest x1 555 us: shards(): summed = lax.psum(one_axis, 'space')]
  transfers between devices with their start and end apart: 17 -> 18, of which waited for: 9 -> 7; matrix products, arithmetic and copies ran while one was open for 9% -> 3% of each run, Pallas kernels for 0% -> 0%
where the time goes in v1:
time: 1770 us; the launch traced here: 1760 us
  waiting for transfers between devices  1010 us (57%)
  blocking collectives  593 us (34%)
  other arithmetic  53.8 us (3%)
  local copies, waits for them, and re-layouts  35.4 us (2%)
  starting transfers between devices  35.1 us (2%)
    psum x1, waiting for transfers between devices, shards(): summed = lax.psum(one_axis, 'space')  993 us
    psum x1, blocking collectives, shards(): summed = lax.psum(one_axis, 'space')  555 us
  transfers between devices with their start and end apart: 18, of which 7 were waited for; matrix products, arithmetic and copies ran while one was open for 3% of the time, Pallas kernels for 0%

profile of v1, /device:TPU:1, one launch (start us, length us, event | category | flops | bytes accessed | tf_op | source)
XLA Modules:
  0.0 1763.1 jit_solution(17184221709993477015)
XLA Ops:
  7.3 1.4 copy.90
  8.7 3.8 collective-permute-start.5
  12.6 11.0 all_gather.12
  24.9 5.4 all_gather.13
  31.5 5.3 all_gather.15
  37.2 1.1 copy.88
  38.3 1.0 copy.89
  39.3 5.4 all_gather.14
  45.0 6.1 collective-permute-start.6
  51.1 0.8 copy.96
  52.0 1.4 fusion.146
  53.4 2.3 fusion.217
  55.7 1.8 copy.94
  57.5 3.4 collective-permute-done.7
  60.9 1.8 copy.97
  62.7 1.2 maximum_maximum_fusion.1
  64.3 1.8 fusion.289
  66.4 11.0 add_convert_fusion
  78.7 2.6 collective-permute-start.13
  81.3 0.8 collective-permute-start.12
  82.1 1.6 maximum_convert_fusion
  83.7 2.9 collective-permute-done.13
  86.5 5.6 collective-permute-done.12
  92.2 1.5 collective-permute-start.14
  93.7 1.0 collective-permute-start.15
  95.2 1.8 collective-permute-done.14
  97.0 2.5 collective-permute-done.15
  100.8 2.2 fusion.120
  103.0 0.8 fusion.294
  103.8 2.9 collective-permute-start
  107.5 1.4 fusion.135
  108.9 1.3 fusion.131
  110.4 2.1 fusion.136
  112.7 5.8 fusion
  118.5 1.2 fusion.137
  119.7 5.3 stack.223
  125.0 1.4 broadcast_multiply_fusion
  126.4 3.4 collective-permute-start.3
  129.9 2.6 collective-permute-start.2
  132.9 3.0 collective-permute-done.3
  136.2 0.7 fusion.288
  137.2 0.7 fusion.287
  138.4 9.1 fusion.139
  147.5 0.8 copy-done.14
  148.3 1.0 fusion.1
  149.4 8.3 fusion.95
  157.6 0.8 fusion.293
  158.5 2.9 collective-permute-start.8
  161.6 0.9 fusion.77
  162.9 10.7 all-reduce.2
  173.5 555.1 %all-reduce = (f32[27,256]{1,0:T(8,128)S(1)}, f32[27,256]{1,0:T(8,128)S(1)}) all-reduce(f32[27,256]{1,0:T(8,128)S(1)} %get-tuple-element.84, f32[27,256]{1,0:T(8,128)S(1)} %get-tuple-element.85), channel_id=1, replica_groups=mesh['own'=2,'space'=128] {'space'}, use_global_device_ids=true, to_apply=%region_32.33 | all-reduce | flops 13824 | bytes 110592 | tf_op jit(solution)/shard_map/psum | solution.py:108
  730.1 1.8 collective-permute-start.11
  732.1 5.2 collective-permute-start.10
  737.3 1.6 fusion.152
  738.9 0.9 copy.107
  739.7 0.9 copy.105
  740.6 1.4 pad_maximum_fusion.2
  742.0 2.0 fusion.286
  744.3 2.1 fusion.285
  746.6 11.5 fusion.138
  758.1 2.1 copy.112
  760.2 992.7 %all-reduce.7.cloned.1.call-done = (f32[256,256]{1,0:T(8,128)}, f32[256,256]{1,0:T(8,128)}) async-done(((f32[256,256]{1,0:T(8,128)}, f32[256,256]{1,0:T(8,128)}), (f32[256,256]{1,0:T(8,128)}, f32[256,256]{1,0:T(8,128)})) %all-reduce.7.cloned.1.call-update) | async-done | bytes 524304 | tf_op jit(solution)/shard_map/psum | solution.py:108
  1752.9 1.6 constant_dynamic-slice_fusion.3
  1754.5 1.6 constant_dynamic-slice_fusion.2
  (336 shorter events, 10.8 us)
Async XLA Ops:
  7.2 5.4 copy-start.74
  7.2 17.7 %copy-start.75 = (bf16[27,128]{1,0:T(8,128)(2,1)S(1)}, bf16[27,128]{1,0:T(8,128)(2,1)}, u32[]{:S(2)}) copy-start(bf16[27,128]{1,0:T(8,128)(2,1)} %param.11) | copy-start | bytes 20740
  7.2 24.3 %copy-start.21 = (bf16[128,256]{1,0:T(8,128)(2,1)S(1)}, bf16[128,256]{1,0:T(8,128)(2,1)}, u32[]{:S(2)}) copy-start(bf16[128,256]{1,0:T(8,128)(2,1)} %param.8) | copy-start | bytes 196612
  7.2 29.6 %copy-start.15 = (bf16[256,2,4,128]{3,2,1,0:T(4,128)(2,1)S(1)}, bf16[256,2,4,128]{3,2,1,0:T(4,128)(2,1)}, u32[]{:S(2)}) copy-start(bf16[256,2,4,128]{3,2,1,0:T(4,128)(2,1)} %param.7) | copy-start | bytes 1572868
  7.2 739.1 %all-reduce.9.cloned.1.call-start = ((), (), s32[]{:S(2)}) async-start(), calls=%async_computation.1 | async-start | bytes 1048576 | tf_op jit(solution)/shard_map/psum | solution.py:107
  8.7 36.1 %collective-permute-start.5 = (bf16[256,1,4,128]{0,3,2,1:T(8,128)(2,1)S(1)}, bf16[256,1,4,128]{0,3,2,1:T(8,128)(2,1)S(1)}, u32[]{:S(2)}, u32[]{:S(2)}) collective-permute-start(bf16[256,1,4,128]{0,3,2,1:T(8,128)(2,1)S(1)} %get-tuple-element.222), channel_id=1, source_target_pairs={{128,0},{0,128},{129,1},{1,129},{130,2},{2,130},{131,3},{3,131},{1... | collective-permute-start | bytes 786440 | tf_op jit(solution)/shard_map/ppermute | solution.py:23
  12.5 32.3 %collective-permute-start.4 = (bf16[256,1,4,128]{0,3,2,1:T(8,128)(2,1)S(1)}, bf16[256,1,4,128]{0,3,2,1:T(8,128)(2,1)S(1)}, u32[]{:S(2)}, u32[]{:S(2)}) collective-permute-start(bf16[256,1,4,128]{0,3,2,1:T(8,128)(2,1)S(1)} %get-tuple-element.221), channel_id=1, source_target_pairs={{0,128},{128,0},{1,129},{129,1},{2,130},{130,2},{3,131},{131,3},{4... | collective-permute-start | bytes 786440 | tf_op jit(solution)/shard_map/ppermute | solution.py:22
  45.0 10.7 collective-permute-start.6
  52.0 8.9 collective-permute-start.7
  53.4 2.3 copy-start.5
  53.4 2.3 copy-start.7
  78.7 7.8 collective-permute-start.13
  81.3 10.8 collective-permute-start.12
  92.2 4.8 collective-permute-start.14
  93.7 5.8 collective-permute-start.15
  103.8 22.6 %collective-permute-start = (bf16[256,1,4,128]{0,3,2,1:T(8,128)(2,1)}, bf16[256,1,4,128]{0,3,2,1:T(8,128)(2,1)S(1)}, u32[]{:S(2)}, u32[]{:S(2)}) collective-permute-start(bf16[256,1,4,128]{0,3,2,1:T(8,128)(2,1)} %get-tuple-element.214), channel_id=1, source_target_pairs={{0,128},{128,0},{1,129},{129,1},{2,130},{130,2},{3,131},{131,3},{4... | collective-permute-start | bytes 786440 | tf_op jit(solution)/shard_map/ppermute | solution.py:22
  106.7 19.7 %collective-permute-start.1 = (bf16[256,1,4,128]{0,3,2,1:T(8,128)(2,1)}, bf16[256,1,4,128]{0,3,2,1:T(8,128)(2,1)S(1)}, u32[]{:S(2)}, u32[]{:S(2)}) collective-permute-start(bf16[256,1,4,128]{0,3,2,1:T(8,128)(2,1)} %get-tuple-element.213), channel_id=1, source_target_pairs={{128,0},{0,128},{129,1},{1,129},{130,2},{2,130},{131,3},{3,131},{1... | collective-permute-start | bytes 786440 | tf_op jit(solution)/shard_map/ppermute | solution.py:23
  110.2 2.3 copy-start.98
  110.2 2.3 copy-start.100
  110.2 2.3 copy-start.102
  110.2 2.3 copy-start.104
  110.2 2.3 copy-start.106
  110.2 2.3 copy-start.108
  110.2 2.3 copy-start.110
  110.2 2.3 copy-start.112
  110.3 2.3 copy-start.114
  110.3 2.3 copy-start.116
  110.3 2.3 copy-start.118
  110.3 2.3 copy-start.120
  110.3 2.3 copy-start.122
  126.4 9.6 collective-permute-start.3
  129.9 6.1 collective-permute-start.2
  138.4 9.9 copy-start.17
  149.4 12.3 copy-start.1
  158.5 571.4 %collective-permute-start.8 = (bf16[256,1,4,128]{0,3,2,1:T(8,128)(2,1)}, bf16[256,1,4,128]{0,3,2,1:T(8,128)(2,1)S(1)}, u32[]{:S(2)}, u32[]{:S(2)}) collective-permute-start(bf16[256,1,4,128]{0,3,2,1:T(8,128)(2,1)} %get-tuple-element.204), channel_id=1, source_target_pairs={{0,128},{128,0},{1,129},{129,1},{2,130},{130,2},{3,131},{131,3},{4... | collective-permute-start | bytes 786440 | tf_op jit(solution)/shard_map/ppermute | solution.py:22
  161.5 568.4 %collective-permute-start.9 = (bf16[256,1,4,128]{0,3,2,1:T(8,128)(2,1)}, bf16[256,1,4,128]{0,3,2,1:T(8,128)(2,1)S(1)}, u32[]{:S(2)}, u32[]{:S(2)}) collective-permute-start(bf16[256,1,4,128]{0,3,2,1:T(8,128)(2,1)} %get-tuple-element.203), channel_id=1, source_target_pairs={{128,0},{0,128},{129,1},{1,129},{130,2},{2,130},{131,3},{3,131},{1... | collective-permute-start | bytes 786440 | tf_op jit(solution)/shard_map/ppermute | solution.py:23
  162.8 1590.1 %all-reduce.7.cloned.1.call-start = ((), (), s32[]{:S(2)}) async-start(), calls=%async_computation | async-start | bytes 1048576 | tf_op jit(solution)/shard_map/psum | solution.py:108
  729.9 9.0 copy-start.4
  730.1 8.7 collective-permute-start.11
  732.1 7.7 collective-permute-start.10
  744.1 2.3 copy-start.24
  744.1 2.3 copy-start.26
  744.1 2.3 copy-start.28
  744.1 2.3 copy-start.30
  744.1 2.4 copy-start.32
  744.1 2.4 copy-start.34
  744.1 2.4 copy-start.36
  744.1 2.4 copy-start.38
  744.1 2.4 copy-start.40
  744.1 2.4 copy-start.42
  744.1 2.4 copy-start.44
  744.1 2.4 copy-start.46
  744.1 2.4 copy-start.48
  744.2 2.4 copy-start.50
  744.2 2.4 copy-start.52
  744.2 2.4 copy-start.54
  744.2 2.4 copy-start.56
  744.2 2.4 copy-start.58
  744.2 2.4 copy-start.60
  744.2 2.4 copy-start.62
  744.2 2.4 copy-start.64
  744.2 2.4 copy-start.66
  744.2 2.4 copy-start.68
  744.3 2.4 copy-start.70
  (98 other events, 165.8 us)
Sparse Core Ops, SparseCore 0:
  162.9 50.6 all-reduce.8
  746.5 1006.3 all-reduce.6
